TPU v7x, 32 devices: a whole 2x2x4 slice. The times are simulated.
32 devices in a mesh: grp: 2 (over y), lon: 4 (over z), view: 4 (over x, core).
Axes of the slice: x: 2, y: 2, z: 4, core: 2. Of those that a mesh axis runs over, the one named last changes fastest.
Arguments:
- light_field: bfloat16 [128, 4, 128, 128], P(('grp', 'view'), None, 'lon'), parts along dimension 0, may hold values from -6 to 6
- spatial_weights: bfloat16 [3, 3, 3, 128, 128], replicated, may hold values from -0.1875 to 0.1875
- spatial_offsets: float32 [3, 128], replicated, may hold values from -3 to 3
- angular_weight: bfloat16 [3, 3, 128, 128], replicated, may hold values from -0.1875 to 0.1875
- angular_offset: float32 [128], replicated, may hold values from -3 to 3
Outputs:
- refined: bfloat16 [128, 4, 128, 128], P(('grp', 'view'), None, 'lon'), parts along dimension 0
There are 2 independent parts, one for each index of `grp`. A program takes and returns all parts, laid end to end along the dimension named above; an argument that names none is the same for every part. Nothing has to cross between parts.
All inputs are finite; a program needn't handle non-finite values.
Results may differ from a plain program's by a relative error of at most 0.0047.
Values may be sent and summed in bfloat16 or wider, within the bound.
A program may use at most 64 MiB of HBM per device.

v0:
```python
import jax
import jax.numpy as jnp
from jax import lax
from jax.sharding import PartitionSpec as P

ANG = 8


def with_halo(cells, sides, width, closed):
    for axis, dim in sides:
        count = lax.axis_size(axis)
        ends = count if closed else count - 1
        head = lax.slice_in_dim(cells, 0, width, axis=dim)
        tail = lax.slice_in_dim(cells, cells.shape[dim] - width, cells.shape[dim], axis=dim)
        cells = jnp.concatenate(
            [
                lax.ppermute(tail, axis, [(i, (i + 1) % count) for i in range(ends)]),
                cells,
                lax.ppermute(head, axis, [((i + 1) % count, i) for i in range(ends)]),
            ],
            axis=dim,
        )
    return cells


def spatial_layer(widened, weight, offset):
    count, rows, wide_cols, chans = widened.shape
    cols = wide_cols - 2
    padded = jnp.pad(widened, ((0, 0), (1, 1), (0, 0), (0, 0)))
    total = jnp.zeros((count * rows * cols, chans), jnp.float32)
    for row_tap in range(3):
        stacked = jnp.concatenate(
            [padded[:, row_tap : row_tap + rows, col_tap : col_tap + cols] for col_tap in range(3)],
            axis=-1,
        )
        total = total + jnp.dot(
            stacked.reshape(-1, 3 * chans),
            weight[row_tap].reshape(3 * chans, chans),
            preferred_element_type=jnp.float32,
        )
    total = total.reshape(count, rows, cols, chans) + offset
    return jax.nn.gelu(total, approximate=True).astype(jnp.bfloat16)


def angular_layer(padded_rows, weight, offset):
    chans = padded_rows.shape[-1]
    grid_rows = padded_rows.shape[0] - 2
    views_grid = padded_rows.reshape(grid_rows + 2, ANG, -1, chans)
    padded = jnp.pad(views_grid, ((0, 0), (1, 1), (0, 0), (0, 0)))
    total = jnp.zeros((grid_rows * ANG * views_grid.shape[2], chans), jnp.float32)
    for row_tap in range(3):
        stacked = jnp.concatenate(
            [
                padded[row_tap : row_tap + grid_rows, col_tap : col_tap + ANG]
                for col_tap in range(3)
            ],
            axis=-1,
        )
        total = total + jnp.dot(
            stacked.reshape(-1, 3 * chans),
            weight[row_tap].reshape(3 * chans, chans),
            preferred_element_type=jnp.float32,
        )
    return (total + offset).astype(jnp.bfloat16)


def local(light_field, spatial_weights, spatial_offsets, angular_weight, angular_offset):
    layer_count = spatial_weights.shape[0]
    hidden = light_field
    for layer_index in range(layer_count):
        widened = with_halo(hidden, (("lon", 2),), 1, True)
        hidden = spatial_layer(widened, spatial_weights[layer_index], spatial_offsets[layer_index])
    chans = hidden.shape[-1]
    grid_rows = hidden.shape[0] // ANG
    shaped = hidden.reshape(grid_rows, ANG, hidden.shape[1], hidden.shape[2], chans)
    bordered = with_halo(shaped, (("view", 0),), 1, False)
    angular = angular_layer(bordered, angular_weight, angular_offset).reshape(hidden.shape)
    angular = lax.optimization_barrier(angular)
    return (light_field.astype(jnp.float32) + angular.astype(jnp.float32)).astype(jnp.bfloat16)


def solution(mesh):
    return jax.shard_map(
        local,
        mesh=mesh,
        in_specs=(P(("grp", "view"), None, "lon", None), P(), P(), P(), P()),
        out_specs=P(("grp", "view"), None, "lon", None),
        check_vma=False,
    )
```

profile of v0, /device:TPU:1, one launch (start us, length us, event | category | flops | bytes accessed | tf_op | source)
XLA Modules:
  0.0 48.9 jit_solution(11546662271457591534)
XLA Ops:
  0.0 1.1 %fusion.68 = (bf16[16,4,1,128]{3,2,1,0:T(2,128)(2,1)S(1)}, bf16[16,4,1,128]{3,2,1,0:T(2,128)(2,1)S(1)}) fusion(bf16[16,4,32,128]{3,2,1,0:T(8,128)(2,1)} %param.5), kind=kLoop, calls=%fused_computation.107 | loop fusion | bytes 65536 | tf_op jit(solution)/shard_map/slice | solution.py:14
  1.1 2.2 %collective-permute-start = (bf16[16,4,1,128]{3,2,1,0:T(2,128)(2,1)S(1)}, bf16[16,4,1,128]{3,2,1,0:T(2,128)(2,1)S(1)}, u32[]{:S(2)}, u32[]{:S(2)}) collective-permute-start(bf16[16,4,1,128]{3,2,1,0:T(2,128)(2,1)S(1)} %get-tuple-element.47), channel_id=1, source_target_pairs={{0,4},{4,8},{8,12},{12,0},{1,5},{5,9},{9,13},{13,1},{2,6},{6,10},{... | collective-permute-start | bytes 49160 | tf_op jit(solution)/shard_map/ppermute | solution.py:17
  3.3 2.1 %collective-permute-start.1 = (bf16[16,4,1,128]{3,2,1,0:T(2,128)(2,1)S(1)}, bf16[16,4,1,128]{3,2,1,0:T(2,128)(2,1)S(1)}, u32[]{:S(2)}, u32[]{:S(2)}) collective-permute-start(bf16[16,4,1,128]{3,2,1,0:T(2,128)(2,1)S(1)} %get-tuple-element.48), channel_id=1, source_target_pairs={{4,0},{8,4},{12,8},{0,12},{5,1},{9,5},{13,9},{1,13},{6,2},{10,6},{... | collective-permute-start | bytes 49160 | tf_op jit(solution)/shard_map/ppermute | solution.py:19
  5.4 1.3 %fusion.65 = (bf16[1,1,3,128,128]{4,3,2,1,0:T(8,128)(2,1)S(1)}, bf16[1,1,3,128,128]{4,3,2,1,0:T(8,128)(2,1)S(1)}, bf16[1,1,3,128,128]{4,3,2,1,0:T(8,128)(2,1)S(1...) fusion(bf16[3,3,3,128,128]{4,3,2,1,0:T(8,128)(2,1)} %param.6), kind=kLoop, calls=%fused_computation.104 | loop fusion | bytes 1769472 | tf_op jit(solution)/shard_map/slice | solution.py:38
  7.1 0.8 %fusion.64 = (bf16[16,4,32,128]{3,2,1,0:T(8,128)(2,1)S(1)}, bf16[16,4,32,128]{3,2,1,0:T(8,128)(2,1)S(1)}, bf16[16,4,32,128]{3,2,1,0:T(8,128)(2,1)S(1)}, bf16[16,...) fusion(bf16[16,6,34,128]{3,2,1,0:T(8,128)(2,1)S(1)} %fusion.60), kind=kLoop, calls=%fused_computation.103 | loop fusion | bytes 6291456 | tf_op jit(solution)/shard_map/slice | solution.py:33
  9.1 0.7 %fusion.12 = bf16[16,4,32,384]{3,2,1,0:T(8,128)(2,1)S(1)} fusion(bf16[16,4,1,128]{3,2,1,0:T(2,128)(2,1)S(1)} %collective-permute-done.1, bf16[16,4,32,128]{3,2,1,0:T(8,128)(2,1)S(1)} %copy-done, bf16[16,4,1,128]{3,2,1,0:T(2,128)(2,1)S(1)} %collective-permute-done), kind=kLoop, calls=%fused_computation.31 | loop fusion | flops 7864320 | bytes 2129920 | tf_op jit(solution)/shard_map/concatenate | solution.py:32
  9.8 0.6 %convolution_add_fusion.7 = f32[2048,128]{1,0:T(8,128)S(1)} fusion(f32[2048,128]{1,0:T(8,128)S(1)} %fusion.70, bf16[2048,384]{1,0:T(8,128)(2,1)S(1)} %bitcast.72, bf16[384,128]{1,0:T(8,128)(2,1)S(1)} %bitcast.96), kind=kOutput, calls=%fused_computation.13 | convolution fusion | flops 201588736 | bytes 3768320 | tf_op jit(solution)/shard_map/dot_general | solution.py:36
  11.4 0.8 %collective-permute-start.2 = (bf16[16,4,1,128]{3,2,1,0:T(2,128)(2,1)S(1)}, bf16[16,4,1,128]{3,2,1,0:T(2,128)(2,1)S(1)}, u32[]{:S(2)}, u32[]{:S(2)}) collective-permute-start(bf16[16,4,1,128]{3,2,1,0:T(2,128)(2,1)S(1)} %get-tuple-element.45), channel_id=1, source_target_pairs={{0,4},{4,8},{8,12},{12,0},{1,5},{5,9},{9,13},{13,1},{2,6},{6,10},{... | collective-permute-start | bytes 49160 | tf_op jit(solution)/shard_map/ppermute | solution.py:17
  12.2 2.5 %collective-permute-start.3 = (bf16[16,4,1,128]{3,2,1,0:T(2,128)(2,1)S(1)}, bf16[16,4,1,128]{3,2,1,0:T(2,128)(2,1)S(1)}, u32[]{:S(2)}, u32[]{:S(2)}) collective-permute-start(bf16[16,4,1,128]{3,2,1,0:T(2,128)(2,1)S(1)} %get-tuple-element.46), channel_id=1, source_target_pairs={{4,0},{8,4},{12,8},{0,12},{5,1},{9,5},{13,9},{1,13},{6,2},{10,6},{... | collective-permute-start | bytes 49160 | tf_op jit(solution)/shard_map/ppermute | solution.py:19
  14.7 1.3 %collective-permute-done.2 = bf16[16,4,1,128]{3,2,1,0:T(2,128)(2,1)S(1)} collective-permute-done((bf16[16,4,1,128]{3,2,1,0:T(2,128)(2,1)S(1)}, bf16[16,4,1,128]{3,2,1,0:T(2,128)(2,1)S(1)}, u32[]{:S(2)}, u32[]{:S(2)}) %collective-permute-start.2) | collective-permute-done | bytes 16416 | tf_op jit(solution)/shard_map/ppermute | solution.py:17
  16.4 0.8 %fusion.63 = (bf16[16,4,32,128]{3,2,1,0:T(8,128)(2,1)S(1)}, bf16[16,4,32,128]{3,2,1,0:T(8,128)(2,1)S(1)}, bf16[16,4,32,128]{3,2,1,0:T(8,128)(2,1)S(1)}, bf16[16,...) fusion(bf16[16,6,34,128]{3,2,1,0:T(8,128)(2,1)S(1)} %fusion.58), kind=kLoop, calls=%fused_computation.102 | loop fusion | bytes 6291456 | tf_op jit(solution)/shard_map/slice | solution.py:33
  18.3 0.7 %fusion.10 = bf16[16,4,32,384]{3,2,1,0:T(8,128)(2,1)S(1)} fusion(bf16[16,4,1,128]{3,2,1,0:T(2,128)(2,1)S(1)} %collective-permute-done.3, bf16[16,4,32,128]{3,2,1,0:T(8,128)(2,1)S(1)} %fusion.26, bf16[16,4,1,128]{3,2,1,0:T(2,128)(2,1)S(1)} %collective-permute-done.2), kind=kLoop, calls=%fused_computation.27 | loop fusion | flops 7864320 | bytes 2129920 | tf_op jit(solution)/shard_map/concatenate | solution.py:32
  20.7 0.7 %collective-permute-start.4 = (bf16[16,4,1,128]{3,2,1,0:T(2,128)(2,1)S(1)}, bf16[16,4,1,128]{3,2,1,0:T(2,128)(2,1)S(1)}, u32[]{:S(2)}, u32[]{:S(2)}) collective-permute-start(bf16[16,4,1,128]{3,2,1,0:T(2,128)(2,1)S(1)} %get-tuple-element.43), channel_id=1, source_target_pairs={{0,4},{4,8},{8,12},{12,0},{1,5},{5,9},{9,13},{13,1},{2,6},{6,10},{... | collective-permute-start | bytes 49160 | tf_op jit(solution)/shard_map/ppermute | solution.py:17
  21.4 3.2 %collective-permute-start.5 = (bf16[16,4,1,128]{3,2,1,0:T(2,128)(2,1)S(1)}, bf16[16,4,1,128]{3,2,1,0:T(2,128)(2,1)S(1)}, u32[]{:S(2)}, u32[]{:S(2)}) collective-permute-start(bf16[16,4,1,128]{3,2,1,0:T(2,128)(2,1)S(1)} %get-tuple-element.44), channel_id=1, source_target_pairs={{4,0},{8,4},{12,8},{0,12},{5,1},{9,5},{13,9},{1,13},{6,2},{10,6},{... | collective-permute-start | bytes 49160 | tf_op jit(solution)/shard_map/ppermute | solution.py:19
  24.6 1.0 %collective-permute-done.4 = bf16[16,4,1,128]{3,2,1,0:T(2,128)(2,1)S(1)} collective-permute-done((bf16[16,4,1,128]{3,2,1,0:T(2,128)(2,1)S(1)}, bf16[16,4,1,128]{3,2,1,0:T(2,128)(2,1)S(1)}, u32[]{:S(2)}, u32[]{:S(2)}) %collective-permute-start.4) | collective-permute-done | bytes 16416 | tf_op jit(solution)/shard_map/ppermute | solution.py:17
  26.0 0.8 %fusion.62 = (bf16[16,4,32,128]{3,2,1,0:T(8,128)(2,1)S(1)}, bf16[16,4,32,128]{3,2,1,0:T(8,128)(2,1)S(1)}, bf16[16,4,32,128]{3,2,1,0:T(8,128)(2,1)S(1)}, bf16[16,...) fusion(bf16[16,6,34,128]{3,2,1,0:T(8,128)(2,1)S(1)} %select_maximum_fusion), kind=kLoop, calls=%fused_computation.101 | loop fusion | bytes 6291456 | tf_op jit(solution)/shard_map/slice | solution.py:33
  27.9 0.7 %fusion.8 = bf16[16,4,32,384]{3,2,1,0:T(8,128)(2,1)S(1)} fusion(bf16[16,4,1,128]{3,2,1,0:T(2,128)(2,1)S(1)} %collective-permute-done.5, bf16[16,4,32,128]{3,2,1,0:T(8,128)(2,1)S(1)} %fusion.34, bf16[16,4,1,128]{3,2,1,0:T(2,128)(2,1)S(1)} %collective-permute-done.4), kind=kLoop, calls=%fused_computation.23 | loop fusion | flops 7864320 | bytes 2129920 | tf_op jit(solution)/shard_map/concatenate | solution.py:32
  29.2 0.6 %convolution_add_fusion.2 = f32[2048,128]{1,0:T(8,128)S(1)} fusion(f32[2048,128]{1,0:T(8,128)S(1)} %convolution_add_fusion.3, bf16[2048,384]{1,0:T(8,128)(2,1)S(1)} %bitcast.68, bf16[384,128]{1,0:T(8,128)(2,1)S(1)} %bitcast.87), kind=kOutput, calls=%fused_computation.8 | convolution fusion | flops 201588736 | bytes 3768320 | tf_op jit(solution)/shard_map/dot_general | solution.py:36
  30.3 6.7 %collective-permute-start.6 = (bf16[1,8,4,32,128]{4,3,2,1,0:T(8,128)(2,1)S(1)}, bf16[1,8,4,32,128]{4,3,2,1,0:T(8,128)(2,1)S(1)}, u32[]{:S(2)}, u32[]{:S(2)}) collective-permute-start(bf16[1,8,4,32,128]{4,3,2,1,0:T(8,128)(2,1)S(1)} %get-tuple-element.42), channel_id=1, source_target_pairs={{0,1},{1,2},{2,3},{4,5},{5,6},{6,7},{8,9},{9,10},{10,11},{12,13},{... | collective-permute-start | bytes 786440 | tf_op jit(solution)/shard_map/ppermute | solution.py:17
  37.0 1.9 %collective-permute-start.7 = (bf16[1,8,4,32,128]{4,3,2,1,0:T(8,128)(2,1)S(1)}, bf16[1,8,4,32,128]{4,3,2,1,0:T(8,128)(2,1)S(1)}, u32[]{:S(2)}, u32[]{:S(2)}) collective-permute-start(bf16[1,8,4,32,128]{4,3,2,1,0:T(8,128)(2,1)S(1)} %get-tuple-element.41), channel_id=1, source_target_pairs={{1,0},{2,1},{3,2},{5,4},{6,5},{7,6},{9,8},{10,9},{11,10},{13,12},{... | collective-permute-start | bytes 786440 | tf_op jit(solution)/shard_map/ppermute | solution.py:19
  39.3 1.0 %collective-permute-done.6 = bf16[1,8,4,32,128]{4,3,2,1,0:T(8,128)(2,1)S(1)} collective-permute-done((bf16[1,8,4,32,128]{4,3,2,1,0:T(8,128)(2,1)S(1)}, bf16[1,8,4,32,128]{4,3,2,1,0:T(8,128)(2,1)S(1)}, u32[]{:S(2)}, u32[]{:S(2)}) %collective-permute-start.6) | collective-permute-done | bytes 262176 | tf_op jit(solution)/shard_map/ppermute | solution.py:17
  40.3 4.4 %collective-permute-done.7 = bf16[1,8,4,32,128]{4,3,2,1,0:T(8,128)(2,1)S(1)} collective-permute-done((bf16[1,8,4,32,128]{4,3,2,1,0:T(8,128)(2,1)S(1)}, bf16[1,8,4,32,128]{4,3,2,1,0:T(8,128)(2,1)S(1)}, u32[]{:S(2)}, u32[]{:S(2)}) %collective-permute-start.7) | collective-permute-done | bytes 262176 | tf_op jit(solution)/shard_map/ppermute | solution.py:19
  45.4 0.8 %fusion.5 = (bf16[2,8,128,384]{3,2,1,0:T(8,128)(2,1)S(1)}, bf16[2,8,128,384]{3,2,1,0:T(8,128)(2,1)S(1)}, bf16[2,8,128,384]{3,2,1,0:T(8,128)(2,1)S(1)}) fusion(bf16[1,8,128,128]{3,2,1,0:T(8,128)(2,1)S(1)} %bitcast.85, bf16[2,8,128,128]{3,2,1,0:T(8,128)(2,1)S(1)} %fusion.50, bf16[2,8,128,128]{3,2,1,0:T(8,128)(2,1)S(1)} %get-tuple-element.10, ...), kind=kLoop, calls=%fused_computation.18 | loop fusion | flops 17301504 | bytes 8912896 | tf_op jit(solution)/shard_map/concatenate | solution.py:52
  48.0 0.9 %add_convert_fusion = bf16[16,4,32,128]{3,2,1,0:T(8,128)(2,1)} fusion(bf16[16,4,32,128]{3,2,1,0:T(8,128)(2,1)S(1)} %bitcast.81, bf16[16,4,32,128]{3,2,1,0:T(8,128)(2,1)S(1)} %copy-done), kind=kLoop, calls=%fused_computation.82 | loop fusion | flops 1048576 | bytes 1572864 | tf_op jit(solution)/shard_map/convert_element_type | solution.py:79
  (41 shorter events, 10.9 us)
Async XLA Ops:
  0.0 6.7 %copy-start = (bf16[16,4,32,128]{3,2,1,0:T(8,128)(2,1)S(1)}, bf16[16,4,32,128]{3,2,1,0:T(8,128)(2,1)}, u32[]{:S(2)}) copy-start(bf16[16,4,32,128]{3,2,1,0:T(8,128)(2,1)} %param.5) | copy-start | bytes 1572868
  0.0 6.7 %copy-start.2 = (f32[3,128]{1,0:T(4,128)S(1)}, f32[3,128]{1,0:T(4,128)}, u32[]{:S(2)}) copy-start(f32[3,128]{1,0:T(4,128)} %param.7) | copy-start | bytes 4612
  1.1 5.6 %collective-permute-start = (bf16[16,4,1,128]{3,2,1,0:T(2,128)(2,1)S(1)}, bf16[16,4,1,128]{3,2,1,0:T(2,128)(2,1)S(1)}, u32[]{:S(2)}, u32[]{:S(2)}) collective-permute-start(bf16[16,4,1,128]{3,2,1,0:T(2,128)(2,1)S(1)} %get-tuple-element.47), channel_id=1, source_target_pairs={{0,4},{4,8},{8,12},{12,0},{1,5},{5,9},{9,13},{13,1},{2,6},{6,10},{... | collective-permute-start | bytes 49160 | tf_op jit(solution)/shard_map/ppermute | solution.py:17
  3.3 3.5 %collective-permute-start.1 = (bf16[16,4,1,128]{3,2,1,0:T(2,128)(2,1)S(1)}, bf16[16,4,1,128]{3,2,1,0:T(2,128)(2,1)S(1)}, u32[]{:S(2)}, u32[]{:S(2)}) collective-permute-start(bf16[16,4,1,128]{3,2,1,0:T(2,128)(2,1)S(1)} %get-tuple-element.48), channel_id=1, source_target_pairs={{4,0},{8,4},{12,8},{0,12},{5,1},{9,5},{13,9},{1,13},{6,2},{10,6},{... | collective-permute-start | bytes 49160 | tf_op jit(solution)/shard_map/ppermute | solution.py:19
  11.4 4.6 %collective-permute-start.2 = (bf16[16,4,1,128]{3,2,1,0:T(2,128)(2,1)S(1)}, bf16[16,4,1,128]{3,2,1,0:T(2,128)(2,1)S(1)}, u32[]{:S(2)}, u32[]{:S(2)}) collective-permute-start(bf16[16,4,1,128]{3,2,1,0:T(2,128)(2,1)S(1)} %get-tuple-element.45), channel_id=1, source_target_pairs={{0,4},{4,8},{8,12},{12,0},{1,5},{5,9},{9,13},{13,1},{2,6},{6,10},{... | collective-permute-start | bytes 49160 | tf_op jit(solution)/shard_map/ppermute | solution.py:17
  12.2 3.9 %collective-permute-start.3 = (bf16[16,4,1,128]{3,2,1,0:T(2,128)(2,1)S(1)}, bf16[16,4,1,128]{3,2,1,0:T(2,128)(2,1)S(1)}, u32[]{:S(2)}, u32[]{:S(2)}) collective-permute-start(bf16[16,4,1,128]{3,2,1,0:T(2,128)(2,1)S(1)} %get-tuple-element.46), channel_id=1, source_target_pairs={{4,0},{8,4},{12,8},{0,12},{5,1},{9,5},{13,9},{1,13},{6,2},{10,6},{... | collective-permute-start | bytes 49160 | tf_op jit(solution)/shard_map/ppermute | solution.py:19
  20.2 4.4 %copy-start.1 = (bf16[3,3,128,128]{3,2,1,0:T(8,128)(2,1)S(1)}, bf16[3,3,128,128]{3,2,1,0:T(8,128)(2,1)}, u32[]{:S(2)}) copy-start(bf16[3,3,128,128]{3,2,1,0:T(8,128)(2,1)} %param.8) | copy-start | bytes 884740
  20.7 5.0 %collective-permute-start.4 = (bf16[16,4,1,128]{3,2,1,0:T(2,128)(2,1)S(1)}, bf16[16,4,1,128]{3,2,1,0:T(2,128)(2,1)S(1)}, u32[]{:S(2)}, u32[]{:S(2)}) collective-permute-start(bf16[16,4,1,128]{3,2,1,0:T(2,128)(2,1)S(1)} %get-tuple-element.43), channel_id=1, source_target_pairs={{0,4},{4,8},{8,12},{12,0},{1,5},{5,9},{9,13},{13,1},{2,6},{6,10},{... | collective-permute-start | bytes 49160 | tf_op jit(solution)/shard_map/ppermute | solution.py:17
  21.4 4.3 %collective-permute-start.5 = (bf16[16,4,1,128]{3,2,1,0:T(2,128)(2,1)S(1)}, bf16[16,4,1,128]{3,2,1,0:T(2,128)(2,1)S(1)}, u32[]{:S(2)}, u32[]{:S(2)}) collective-permute-start(bf16[16,4,1,128]{3,2,1,0:T(2,128)(2,1)S(1)} %get-tuple-element.44), channel_id=1, source_target_pairs={{4,0},{8,4},{12,8},{0,12},{5,1},{9,5},{13,9},{1,13},{6,2},{10,6},{... | collective-permute-start | bytes 49160 | tf_op jit(solution)/shard_map/ppermute | solution.py:19
  30.3 10.0 %collective-permute-start.6 = (bf16[1,8,4,32,128]{4,3,2,1,0:T(8,128)(2,1)S(1)}, bf16[1,8,4,32,128]{4,3,2,1,0:T(8,128)(2,1)S(1)}, u32[]{:S(2)}, u32[]{:S(2)}) collective-permute-start(bf16[1,8,4,32,128]{4,3,2,1,0:T(8,128)(2,1)S(1)} %get-tuple-element.42), channel_id=1, source_target_pairs={{0,1},{1,2},{2,3},{4,5},{5,6},{6,7},{8,9},{9,10},{10,11},{12,13},{... | collective-permute-start | bytes 786440 | tf_op jit(solution)/shard_map/ppermute | solution.py:17
  37.0 7.7 %collective-permute-start.7 = (bf16[1,8,4,32,128]{4,3,2,1,0:T(8,128)(2,1)S(1)}, bf16[1,8,4,32,128]{4,3,2,1,0:T(8,128)(2,1)S(1)}, u32[]{:S(2)}, u32[]{:S(2)}) collective-permute-start(bf16[1,8,4,32,128]{4,3,2,1,0:T(8,128)(2,1)S(1)} %get-tuple-element.41), channel_id=1, source_target_pairs={{1,0},{2,1},{3,2},{5,4},{6,5},{7,6},{9,8},{10,9},{11,10},{13,12},{... | collective-permute-start | bytes 786440 | tf_op jit(solution)/shard_map/ppermute | solution.py:19
  46.7 0.7 %copy-start.3 = (f32[128]{0:T(128)S(1)}, f32[128]{0:T(128)}, u32[]{:S(2)}) copy-start(f32[128]{0:T(128)} %param.9) | copy-start | bytes 1540
where the time goes:
time: 49.2 us; the launch traced here: 48.9 us
  starting transfers between devices  20.1 us (41%)
  other arithmetic  8.17 us (17%)
  waiting for transfers between devices  7.73 us (16%)
  matrix products  6.91 us (14%)
  local copies, waits for them, and re-layouts  5.68 us (12%)
    ppermute x4, starting transfers between devices, with_halo(): lax.ppermute(tail, axis, [(i, (i + 1) % count) for i in range(ends)])  10.3 us
    ppermute x4, starting transfers between devices, with_halo(): lax.ppermute(head, axis, [((i + 1) % count, i) for i in range(ends)])  9.78 us
    dot_general x9, matrix products, spatial_layer(): jnp.dot(stacked.reshape(-1, 3 * chans), weight[row_tap].reshape(3 * chans...  5.19 us
    ppermute x4, waiting for transfers between devices, with_halo(): lax.ppermute(head, axis, [((i + 1) % count, i) for i in range(ends)])  4.4 us
    concatenate x8, other arithmetic, spatial_layer(): jnp.concatenate([padded[:, row_tap:row_tap + rows, col_tap:col_tap + cols...  3.64 us
    ppermute x4, waiting for transfers between devices, with_halo(): lax.ppermute(tail, axis, [(i, (i + 1) % count) for i in range(ends)])  3.32 us
    slice x3, local copies, waits for them, and re-layouts, spatial_layer(): padded[:, row_tap:row_tap + rows, col_tap:col_tap + cols]  2.44 us
    dot_general x3, matrix products, angular_layer(): jnp.dot(stacked.reshape(-1, 3 * chans), weight[row_tap].reshape(3 * chans...  1.73 us
  transfers between devices with their start and end apart: 8, of which 4 were waited for; matrix products, arithmetic and copies ran while one was open for 4% of the time, Pallas kernels for 0%

commit v1 on v0

v1 whole, which is shorter than its diff:
```python
import functools

import jax
import jax.numpy as jnp
from jax import lax
from jax.experimental import pallas as pl
from jax.experimental.pallas import tpu as pltpu
from jax.sharding import PartitionSpec as P

ANG = 8
F32 = jnp.float32
BF16 = jnp.bfloat16


def gelu(t):
    return 0.5 * t * (1.0 + jnp.tanh(0.7978845608 * (t + 0.044715 * (t * t * t))))


def kernel(lon_count, view_count, lf, sw, so, aw, ao, out, lfv, x0, x1, x2, flip, hid, wide, awide, acc,
           in_sem, w_sem, lon_send, lon_recv, view_send, view_recv):
    views, rows, cols, chans = lf.shape
    layers = sw.shape[0]
    grid_rows = views // ANG
    pairs = rows // 2
    lon = lax.axis_index("lon")
    view = lax.axis_index("view")
    right, left = lax.rem(lon + 1, lon_count), lax.rem(lon + lon_count - 1, lon_count)
    has_low, has_high = view > 0, view < view_count - 1

    loads = [pltpu.make_async_copy(lf.at[:, r], lfv.at[:, r], in_sem.at[r]) for r in range(rows)]
    for load in loads:
        load.start()
    weights = []
    for l in range(layers):
        weights.append((
            pltpu.make_async_copy(sw.at[l], wide.at[l, 0:3, :, :, 0:chans], w_sem.at[l, 0]),
            pltpu.make_async_copy(sw.at[l], wide.at[l, 1:4, :, :, chans:2 * chans], w_sem.at[l, 1]),
        ))
    weights.append((
        pltpu.make_async_copy(aw, awide.at[:, 0:3, :, 0:chans], w_sem.at[layers, 0]),
        pltpu.make_async_copy(aw, awide.at[:, 1:4, :, chans:2 * chans], w_sem.at[layers, 1]),
    ))
    for both in weights:
        for copy in both:
            copy.start()

    barrier = pltpu.get_barrier_semaphore()
    for neighbour in (left, right):
        pl.semaphore_signal(barrier, inc=1, device_id={"lon": neighbour}, device_id_type=pl.DeviceIdType.MESH)

    @pl.when(has_low)
    def _():
        pl.semaphore_signal(barrier, inc=1, device_id={"view": view - 1}, device_id_type=pl.DeviceIdType.MESH)

    @pl.when(has_high)
    def _():
        pl.semaphore_signal(barrier, inc=1, device_id={"view": view + 1}, device_id_type=pl.DeviceIdType.MESH)

    blank = jnp.zeros((3, chans, chans), BF16)
    for l in range(layers):
        wide[l, 0, :, :, chans:2 * chans] = blank
        wide[l, 3, :, :, 0:chans] = blank
    awide[:, 0, :, chans:2 * chans] = blank
    awide[:, 3, :, 0:chans] = blank

    @pl.when(jnp.logical_not(has_low))
    def _():
        hid[0] = jnp.zeros(hid.shape[1:], BF16)

    @pl.when(jnp.logical_not(has_high))
    def _():
        hid[grid_rows + 1] = jnp.zeros(hid.shape[1:], BF16)

    for r in range(rows):
        loads[r].wait()
        for v in range(views):
            flip[r, pl.ds(v, cols, stride=views), :] = lfv[v, r].astype(F32)
        x0[r, 3 * views:(cols + 3) * views, :] = flip[r].astype(BF16)

    pl.semaphore_wait(barrier, 2 + has_low.astype(jnp.int32) + has_high.astype(jnp.int32))
    to_left = pltpu.make_async_remote_copy(
        src_ref=x0.at[:, 3 * views:6 * views], dst_ref=x0.at[:, (cols + 3) * views:(cols + 6) * views],
        send_sem=lon_send.at[0], recv_sem=lon_recv.at[0],
        device_id={"lon": left}, device_id_type=pl.DeviceIdType.MESH)
    to_right = pltpu.make_async_remote_copy(
        src_ref=x0.at[:, cols * views:(cols + 3) * views], dst_ref=x0.at[:, 0:3 * views],
        send_sem=lon_send.at[1], recv_sem=lon_recv.at[1],
        device_id={"lon": right}, device_id_type=pl.DeviceIdType.MESH)
    to_left.start()
    to_right.start()

    def layer(l, src, p, spans):
        low = max(2 * p - 1, 0)
        high = min(2 * p + 3, rows)
        first, last = low - (2 * p - 1), high - (2 * p - 1)
        taps = []
        for row in range(low, high):
            for b in range(3):
                pieces = [src[row, (s + b) * views:(e + b) * views, :] for s, e in spans]
                taps.append(pieces[0] if len(pieces) == 1 else jnp.concatenate(pieces, axis=0))
        stacked = jnp.concatenate(taps, axis=1)
        weight = wide[l, first:last].reshape((last - first) * 3 * chans, 2 * chans)
        total = jnp.dot(stacked, weight, preferred_element_type=F32)
        offset = so[l:l + 1, :]
        return [gelu(total[:, h * chans:(h + 1) * chans] + offset) for h in range(2)]

    for copy in weights[0]:
        copy.wait()
    for p in range(pairs):
        for h, value in enumerate(layer(0, x0, p, ((3, cols + 1),))):
            x1[2 * p + h, 3 * views:(cols + 1) * views, :] = value.astype(BF16)
    to_left.wait()
    to_right.wait()
    for p in range(pairs):
        for h, value in enumerate(layer(0, x0, p, ((0, 3), (cols + 1, cols + 4)))):
            value = value.astype(BF16)
            x1[2 * p + h, 0:3 * views, :] = value[:3 * views]
            x1[2 * p + h, (cols + 1) * views:(cols + 4) * views, :] = value[3 * views:]
    for copy in weights[1]:
        copy.wait()
    for p in range(pairs):
        for h, value in enumerate(layer(1, x1, p, ((0, cols + 2),))):
            x2[2 * p + h] = value.astype(BF16)
    for copy in weights[2]:
        copy.wait()

    ups, downs = [], []
    for p in range(pairs):
        for h, value in enumerate(layer(2, x2, p, ((0, cols),))):
            r = 2 * p + h
            flip[r] = value
            for v in range(views):
                hid[1 + v // ANG, v % ANG, r * cols:(r + 1) * cols, :] = (
                    flip[r, pl.ds(v, cols, stride=views), :].astype(BF16))
        span = slice(2 * p * cols, (2 * p + 2) * cols)
        ups.append(pltpu.make_async_remote_copy(
            src_ref=hid.at[grid_rows, :, span], dst_ref=hid.at[0, :, span],
            send_sem=view_send.at[0, p], recv_sem=view_recv.at[0, p],
            device_id={"view": view + 1}, device_id_type=pl.DeviceIdType.MESH))
        downs.append(pltpu.make_async_remote_copy(
            src_ref=hid.at[1, :, span], dst_ref=hid.at[grid_rows + 1, :, span],
            send_sem=view_send.at[1, p], recv_sem=view_recv.at[1, p],
            device_id={"view": view - 1}, device_id_type=pl.DeviceIdType.MESH))

        @pl.when(has_high)
        def _(copy=ups[-1]):
            copy.start()

        @pl.when(has_low)
        def _(copy=downs[-1]):
            copy.start()

    for copy in weights[3]:
        copy.wait()

    def partial(u, q, near):
        lo, hi = max(2 * q - 1, 0), min(2 * q + 3, ANG)
        first, last = lo - (2 * q - 1), hi - (2 * q - 1)
        lhs, rhs = [], []
        for a in range(3):
            if (1 <= u + a <= grid_rows) != near:
                continue
            lhs.extend(hid[u + a, v] for v in range(lo, hi))
            rhs.append(awide[a, first:last].reshape((last - first) * chans, 2 * chans))
        return jnp.dot(jnp.concatenate(lhs, axis=1), jnp.concatenate(rhs, axis=0), preferred_element_type=F32)

    for u in range(grid_rows):
        for q in range(ANG // 2):
            acc[u, q] = partial(u, q, True)

    @pl.when(has_low)
    def _():
        for copy in ups:
            copy.wait_recv()

    @pl.when(has_high)
    def _():
        for copy in downs:
            copy.wait_recv()

    offset = ao[...]
    for u in range(grid_rows):
        for q in range(ANG // 2):
            total = acc[u, q]
            if u == 0 or u == grid_rows - 1:
                total = total + partial(u, q, False)
            for h in range(2):
                v = u * ANG + 2 * q + h
                angular = (total[:, h * chans:(h + 1) * chans] + offset).astype(BF16).astype(F32)
                own = lfv[v].reshape(rows * cols, chans).astype(F32)
                out[v] = (own + angular).astype(BF16).reshape(rows, cols, chans)

    @pl.when(has_high)
    def _():
        for copy in ups:
            copy.wait_send()

    @pl.when(has_low)
    def _():
        for copy in downs:
            copy.wait_send()


def local(lon_count, view_count, lf, sw, so, aw, ao):
    views, rows, cols, chans = lf.shape
    layers = sw.shape[0]
    grid_rows = views // ANG
    pairs = rows // 2
    hbm = pl.BlockSpec(memory_space=pl.ANY)
    vmem = pl.BlockSpec(memory_space=pltpu.VMEM)
    return pl.pallas_call(
        functools.partial(kernel, lon_count, view_count),
        out_shape=jax.ShapeDtypeStruct(lf.shape, BF16),
        in_specs=[hbm, hbm, vmem, hbm, vmem],
        out_specs=vmem,
        scratch_shapes=[
            pltpu.VMEM(lf.shape, BF16),
            pltpu.VMEM((rows, (cols + 6) * views, chans), BF16),
            pltpu.VMEM((rows, (cols + 4) * views, chans), BF16),
            pltpu.VMEM((rows, (cols + 2) * views, chans), BF16),
            pltpu.VMEM((rows, cols * views, chans), F32),
            pltpu.VMEM((grid_rows + 2, ANG, rows * cols, chans), BF16),
            pltpu.VMEM((layers, 4, 3, chans, 2 * chans), BF16),
            pltpu.VMEM((3, 4, chans, 2 * chans), BF16),
            pltpu.VMEM((grid_rows, ANG // 2, rows * cols, 2 * chans), F32),
            pltpu.SemaphoreType.DMA((rows,)),
            pltpu.SemaphoreType.DMA((layers + 1, 2)),
            pltpu.SemaphoreType.DMA((2,)),
            pltpu.SemaphoreType.DMA((2,)),
            pltpu.SemaphoreType.DMA((2, pairs)),
            pltpu.SemaphoreType.DMA((2, pairs)),
        ],
        compiler_params=pltpu.CompilerParams(collective_id=0, has_side_effects=True),
    )(lf, sw, so, aw, ao.reshape(1, chans))


def solution(mesh):
    return jax.shard_map(
        functools.partial(local, mesh.shape["lon"], mesh.shape["view"]),
        mesh=mesh,
        in_specs=(P(("grp", "view"), None, "lon", None), P(), P(), P(), P()),
        out_specs=P(("grp", "view"), None, "lon", None),
        check_vma=False,
    )
```

time: 49.2 us -> 21.5 us (0.44)
  starting transfers between devices: 20.1 us -> 0 us
  Pallas kernels: 0 us -> 19.4 us
  other arithmetic: 8.17 us -> 0 us
  waiting for transfers between devices: 7.73 us -> 0 us
  matrix products: 6.91 us -> 0 us
  local copies, waits for them, and re-layouts: 5.68 us -> 1.88 us
    ppermute x8 -> x0, starting transfers between devices: 20.1 us -> none  [the longest x4 10.3 us: with_halo(): lax.ppermute(tail, axis, [(i, (i + 1) % count) for i in range(ends)])]
    pallas_call x0 -> x1, Pallas kernels: none -> 19.4 us  [local(): pl.pallas_call(functools.partial(kernel, lon_count, view_count), out_shap...]
    ppermute x8 -> x0, waiting for transfers between devices: 7.73 us -> none  [the longest x4 4.4 us: with_halo(): lax.ppermute(head, axis, [((i + 1) % count, i) for i in range(ends)])]
    dot_general x12 -> x0, matrix products: 6.91 us -> none  [the longest x9 5.19 us: spatial_layer(): jnp.dot(stacked.reshape(-1, 3 * chans), weight[row_tap].reshape(3 * chans...]
    concatenate x13 -> x0, other arithmetic: 5.69 us -> none  [the longest x8 3.64 us: spatial_layer(): jnp.concatenate([padded[:, row_tap:row_tap + rows, col_tap:col_tap + cols...]
    slice x10 -> x0, local copies, waits for them, and re-layouts: 5.59 us -> none  [the longest x3 2.44 us: spatial_layer(): padded[:, row_tap:row_tap + rows, col_tap:col_tap + cols]]
    convert_element_type x5 -> x0, other arithmetic: 2.48 us -> none  [the longest x4 1.53 us: spatial_layer(): return jax.nn.gelu(total, approximate=True).astype(jnp.bfloat16)]
    unnamed x8 -> x1, local copies, waits for them, and re-layouts: 0.08 us -> 1.88 us
  transfers between devices with their start and end apart: 8 -> 0, of which waited for: 4 -> 0; matrix products, arithmetic and copies ran while one was open for 4% -> 0% of each run, Pallas kernels for 0% -> 0%
where the time goes in v1:
time: 21.5 us; the launch traced here: 21.3 us
  Pallas kernels  19.4 us (90%)
  local copies, waits for them, and re-layouts  1.88 us (9%)
    pallas_call x1, Pallas kernels, local(): pl.pallas_call(functools.partial(kernel, lon_count, view_count), out_shap...  19.4 us
    unnamed x1, local copies, waits for them, and re-layouts  1.88 us

profile of v1, /device:TPU:1, one launch (start us, length us, event | category | flops | bytes accessed | tf_op | source)
XLA Modules:
  0.0 21.3 jit_solution(2029626612169622661)
XLA Ops:
  0.0 19.4 %shard_map.55 = bf16[16,4,32,128]{3,2,1,0:T(8,128)(2,1)} custom-call(bf16[16,4,32,128]{3,2,1,0:T(8,128)(2,1)} %lf.1, bf16[3,3,3,128,128]{4,3,2,1,0:T(8,128)(2,1)} %sw.1, f32[3,128]{1,0:T(4,128)} %so.1, bf16[3,3,128,128]{3,2,1,0:T(8,128)(2,1)} %aw.1, f32[1,128]{1,0:T(1,128)} %bitcast.1), custom_call_target="tpu_custom_call" | custom-call | tf_op jit(solution)/shard_map/pallas_call | solution.py:211
  19.4 1.9 %copy.7 = bf16[16,4,32,128]{3,2,1,0:T(8,128)(2,1)} copy(bf16[16,4,32,128]{3,2,1,0:T(8,128)(2,1)} %shard_map.55) | data formatting | bytes 1048576

commit v2 on v1

v2 whole, which is shorter than its diff:
```python
import functools

import jax
import jax.numpy as jnp
from jax import lax
from jax.experimental import pallas as pl
from jax.experimental.pallas import tpu as pltpu
from jax.sharding import PartitionSpec as P

ANG = 8
EDGE = 4
F32 = jnp.float32
BF16 = jnp.bfloat16


def gelu(t):
    return 0.5 * t * (1.0 + jnp.tanh(0.7978845608 * (t + 0.044715 * (t * t * t))))


def kernel(lon_count, view_count, lf, sw, so_hbm, aw, ao_hbm, out, so, ao, lfv, x0, x1, x2, flip, flip_edge, hid, hid_edge, wide, awide,
           acc, acc_edge, full,
           in_sem, w_sem, b_sem, lon_send, lon_recv, view_send, view_recv):
    views, rows, cols, chans = lf.shape
    layers = sw.shape[0]
    grid_rows = views // ANG
    pairs = rows // 2
    lon = lax.axis_index("lon")
    view = lax.axis_index("view")
    right, left = lax.rem(lon + 1, lon_count), lax.rem(lon + lon_count - 1, lon_count)
    has_low, has_high = view > 0, view < view_count - 1

    barrier = pltpu.get_barrier_semaphore()
    for neighbour in (left, right):
        pl.semaphore_signal(barrier, inc=1, device_id={"lon": neighbour}, device_id_type=pl.DeviceIdType.MESH)

    @pl.when(has_low)
    def _():
        pl.semaphore_signal(barrier, inc=1, device_id={"view": view - 1}, device_id_type=pl.DeviceIdType.MESH)

    @pl.when(has_high)
    def _():
        pl.semaphore_signal(barrier, inc=1, device_id={"view": view + 1}, device_id_type=pl.DeviceIdType.MESH)

    loads = [pltpu.make_async_copy(lf.at[:, r], lfv.at[:, r], in_sem.at[r]) for r in range(rows)]
    for load in loads:
        load.start()
    biases = [pltpu.make_async_copy(so_hbm, so, b_sem.at[0]), pltpu.make_async_copy(ao_hbm, ao, b_sem.at[1])]
    for copy in biases:
        copy.start()
    weights = []
    for l in range(layers):
        weights.append((
            pltpu.make_async_copy(sw.at[l], wide.at[l, 0:3, :, :, 0:chans], w_sem.at[l, 0]),
            pltpu.make_async_copy(sw.at[l], wide.at[l, 1:4, :, :, chans:2 * chans], w_sem.at[l, 1]),
        ))
    weights.append((
        pltpu.make_async_copy(aw, awide.at[:, 0:3, :, 0:chans], w_sem.at[layers, 0]),
        pltpu.make_async_copy(aw, awide.at[:, 1:4, :, chans:2 * chans], w_sem.at[layers, 1]),
    ))
    for both in weights:
        for copy in both:
            copy.start()

    blank = jnp.zeros((3, chans, chans), BF16)
    for l in range(layers):
        wide[l, 0, :, :, chans:2 * chans] = blank
        wide[l, 3, :, :, 0:chans] = blank
    awide[:, 0, :, chans:2 * chans] = blank
    awide[:, 3, :, 0:chans] = blank

    @pl.when(jnp.logical_not(has_low))
    def _():
        hid[0] = jnp.zeros(hid.shape[1:], BF16)
        hid_edge[0] = jnp.zeros(hid_edge.shape[1:], BF16)

    @pl.when(jnp.logical_not(has_high))
    def _():
        hid[grid_rows + 1] = jnp.zeros(hid.shape[1:], BF16)
        hid_edge[grid_rows + 1] = jnp.zeros(hid_edge.shape[1:], BF16)

    for x in (x0, x1, x2):
        x[0] = jnp.zeros(x.shape[1:], BF16)
        x[rows + 1] = jnp.zeros(x.shape[1:], BF16)

    for r in range(rows):
        loads[r].wait()
        for v in range(views):
            flip[r, pl.ds(v, cols, stride=views), :] = lfv[v, r].astype(F32)
        x0[r + 1, 3 * views:(cols + 3) * views, :] = flip[r].astype(BF16)

    def activate(l, total):
        offset = so[l:l + 1, :]
        return [gelu(total[:, h * chans:(h + 1) * chans] + offset) for h in range(2)]

    def inner(l, src, p, start, end):
        low, high = max(2 * p, 1), min(2 * p + 4, rows + 1)
        first, last = low - 2 * p, high - 2 * p
        taps = [src[row, (start + b) * views:(end + b) * views, :] for row in range(low, high) for b in range(3)]
        weight = wide[l, first:last].reshape((last - first) * 3 * chans, 2 * chans)
        return activate(l, jnp.dot(jnp.concatenate(taps, axis=1), weight, preferred_element_type=F32))

    def outer(l, src, spans):
        taps = []
        for i in range(4):
            for b in range(3):
                taps.append(jnp.concatenate(
                    [src[2 * p + i, (s + b) * views:(e + b) * views, :] for p in range(pairs) for s, e in spans], axis=0))
        weight = wide[l].reshape(12 * chans, 2 * chans)
        return activate(l, jnp.dot(jnp.concatenate(taps, axis=1), weight, preferred_element_type=F32))

    def store_outer(dst, values, width):
        side = 3 * views
        for h, value in enumerate(values):
            value = value.astype(BF16)
            for p in range(pairs):
                dst[2 * p + h + 1, 0:side, :] = value[2 * p * side:(2 * p + 1) * side]
                dst[2 * p + h + 1, (width - 3) * views:width * views, :] = value[(2 * p + 1) * side:(2 * p + 2) * side]

    def view_copies(ref, k, span):
        up = pltpu.make_async_remote_copy(
            src_ref=ref.at[grid_rows, :, span], dst_ref=ref.at[0, :, span],
            send_sem=view_send.at[0, k], recv_sem=view_recv.at[0, k],
            device_id={"view": view + 1}, device_id_type=pl.DeviceIdType.MESH)
        down = pltpu.make_async_remote_copy(
            src_ref=ref.at[1, :, span], dst_ref=ref.at[grid_rows + 1, :, span],
            send_sem=view_send.at[1, k], recv_sem=view_recv.at[1, k],
            device_id={"view": view - 1}, device_id_type=pl.DeviceIdType.MESH)

        @pl.when(has_high)
        def _():
            up.start()

        @pl.when(has_low)
        def _():
            down.start()

        return up, down

    def receive(copies):
        @pl.when(has_low)
        def _():
            for up, _ in copies:
                up.wait_recv()

        @pl.when(has_high)
        def _():
            for _, down in copies:
                down.wait_recv()

    for copy in biases:
        copy.wait()
    for copy in weights[0]:
        copy.wait()
    for p in range(pairs):
        for h, value in enumerate(inner(0, x0, p, 3, cols + 1)):
            x1[2 * p + h + 1, 3 * views:(cols + 1) * views, :] = value.astype(BF16)
    for copy in weights[1]:
        copy.wait()
    for p in range(pairs):
        for h, value in enumerate(inner(1, x1, p, 3, cols - 1)):
            x2[2 * p + h + 1, 3 * views:(cols - 1) * views, :] = value.astype(BF16)

    pl.semaphore_wait(barrier, 2 + has_low.astype(jnp.int32) + has_high.astype(jnp.int32))
    to_left = pltpu.make_async_remote_copy(
        src_ref=x0.at[1:rows + 1, 3 * views:6 * views],
        dst_ref=x0.at[1:rows + 1, (cols + 3) * views:(cols + 6) * views],
        send_sem=lon_send.at[0], recv_sem=lon_recv.at[0],
        device_id={"lon": left}, device_id_type=pl.DeviceIdType.MESH)
    to_right = pltpu.make_async_remote_copy(
        src_ref=x0.at[1:rows + 1, cols * views:(cols + 3) * views], dst_ref=x0.at[1:rows + 1, 0:3 * views],
        send_sem=lon_send.at[1], recv_sem=lon_recv.at[1],
        device_id={"lon": right}, device_id_type=pl.DeviceIdType.MESH)
    to_left.start()
    to_right.start()

    for copy in weights[2]:
        copy.wait()
    middle = cols - 2 * EDGE
    sent = []
    for p in range(pairs):
        for h, value in enumerate(inner(2, x2, p, EDGE, cols - EDGE)):
            flip[2 * p + h, 0:middle * views] = value
        for v in range(views):
            both = [flip[2 * p + h, pl.ds(v, middle, stride=views), :] for h in range(2)]
            hid[1 + v // ANG, v % ANG, 2 * p * middle:(2 * p + 2) * middle, :] = (
                jnp.concatenate(both, axis=0).astype(BF16))
        sent.append(view_copies(hid, p, slice(2 * p * middle, (2 * p + 2) * middle)))
    for copy in weights[3]:
        copy.wait()

    def partial(ref, u, q, near):
        lo, hi = max(2 * q - 1, 0), min(2 * q + 3, ANG)
        first, last = lo - (2 * q - 1), hi - (2 * q - 1)
        lhs, rhs = [], []
        for a in range(3):
            if (1 <= u + a <= grid_rows) != near:
                continue
            lhs.extend(ref[u + a, v] for v in range(lo, hi))
            rhs.append(awide[a, first:last].reshape((last - first) * chans, 2 * chans))
        return jnp.dot(jnp.concatenate(lhs, axis=1), jnp.concatenate(rhs, axis=0), preferred_element_type=F32)

    blocks = [(u, q) for u in range(grid_rows) for q in range(ANG // 2)]

    def finish(ref, sums, put):
        for u, q in blocks:
            total = sums[u, q]
            if u == 0 or u == grid_rows - 1:
                total = total + partial(ref, u, q, False)
            for h in range(2):
                value = total[:, h * chans:(h + 1) * chans] + ao[...]
                for r in range(rows):
                    put(u * ANG + 2 * q + h, r, value)

    def put_middle(v, r, value):
        full[v, r * cols + EDGE:(r + 1) * cols - EDGE, :] = value[r * middle:(r + 1) * middle]

    def put_edge(v, r, value):
        start = 2 * EDGE * r
        full[v, r * cols:r * cols + EDGE, :] = value[start:start + EDGE]
        full[v, (r + 1) * cols - EDGE:(r + 1) * cols, :] = value[start + EDGE:start + 2 * EDGE]

    for u, q in blocks:
        acc[u, q] = partial(hid, u, q, True)

    to_left.wait()
    to_right.wait()
    store_outer(x1, outer(0, x0, ((0, 3), (cols + 1, cols + 4))), cols + 4)
    store_outer(x2, outer(1, x1, ((0, 3), (cols - 1, cols + 2))), cols + 2)
    span = 2 * EDGE * views
    for h, value in enumerate(outer(2, x2, ((0, EDGE), (cols - EDGE, cols)))):
        for p in range(pairs):
            flip_edge[2 * p + h] = value[p * span:(p + 1) * span]
    for v in range(views):
        for p in range(pairs):
            both = [flip_edge[2 * p + h, pl.ds(v, 2 * EDGE, stride=views), :] for h in range(2)]
            hid_edge[1 + v // ANG, v % ANG, 4 * EDGE * p:4 * EDGE * (p + 1), :] = (
                jnp.concatenate(both, axis=0).astype(BF16))
    last_sent = view_copies(hid_edge, pairs, slice(0, 2 * EDGE * rows))

    receive(sent)
    finish(hid, acc, put_middle)
    for u, q in blocks:
        acc_edge[u, q] = partial(hid_edge, u, q, True)
    receive([last_sent])
    finish(hid_edge, acc_edge, put_edge)
    for v in range(views):
        out[v] = full[v].astype(BF16).reshape(rows, cols, chans)

    @pl.when(has_high)
    def _():
        for up, _ in sent + [last_sent]:
            up.wait_send()

    @pl.when(has_low)
    def _():
        for _, down in sent + [last_sent]:
            down.wait_send()


def local(lon_count, view_count, lf, sw, so, aw, ao):
    views, rows, cols, chans = lf.shape
    layers = sw.shape[0]
    grid_rows = views // ANG
    pairs = rows // 2
    hbm = pl.BlockSpec(memory_space=pltpu.HBM)
    vmem = pl.BlockSpec(memory_space=pltpu.VMEM)
    angular = pl.pallas_call(
        functools.partial(kernel, lon_count, view_count),
        out_shape=jax.ShapeDtypeStruct(lf.shape, BF16),
        in_specs=[hbm] * 5,
        out_specs=vmem,
        scratch_shapes=[
            pltpu.VMEM(so.shape, F32),
            pltpu.VMEM((1, chans), F32),
            pltpu.VMEM(lf.shape, BF16),
            pltpu.VMEM((rows + 2, (cols + 6) * views, chans), BF16),
            pltpu.VMEM((rows + 2, (cols + 4) * views, chans), BF16),
            pltpu.VMEM((rows + 2, (cols + 2) * views, chans), BF16),
            pltpu.VMEM((rows, cols * views, chans), F32),
            pltpu.VMEM((rows, 2 * EDGE * views, chans), F32),
            pltpu.VMEM((grid_rows + 2, ANG, rows * (cols - 2 * EDGE), chans), BF16),
            pltpu.VMEM((grid_rows + 2, ANG, rows * 2 * EDGE, chans), BF16),
            pltpu.VMEM((layers, 4, 3, chans, 2 * chans), BF16),
            pltpu.VMEM((3, 4, chans, 2 * chans), BF16),
            pltpu.VMEM((grid_rows, ANG // 2, rows * (cols - 2 * EDGE), 2 * chans), F32),
            pltpu.VMEM((grid_rows, ANG // 2, rows * 2 * EDGE, 2 * chans), F32),
            pltpu.VMEM((views, rows * cols, chans), F32),
            pltpu.SemaphoreType.DMA((rows,)),
            pltpu.SemaphoreType.DMA((layers + 1, 2)),
            pltpu.SemaphoreType.DMA((2,)),
            pltpu.SemaphoreType.DMA((2,)),
            pltpu.SemaphoreType.DMA((2,)),
            pltpu.SemaphoreType.DMA((2, pairs + 1)),
            pltpu.SemaphoreType.DMA((2, pairs + 1)),
        ],
        compiler_params=pltpu.CompilerParams(collective_id=0, has_side_effects=True, vmem_limit_bytes=60 * 1024 * 1024),
    )(lf, sw, so, aw, ao.reshape(1, chans))
    return (lf.astype(F32) + angular.astype(F32)).astype(BF16)


def solution(mesh):
    return jax.shard_map(
        functools.partial(local, mesh.shape["lon"], mesh.shape["view"]),
        mesh=mesh,
        in_specs=(P(("grp", "view"), None, "lon", None), P(), P(), P(), P()),
        out_specs=P(("grp", "view"), None, "lon", None),
        check_vma=False,
    )
```

time: 21.5 us -> 19.7 us (0.916)
  other arithmetic: 0 us -> 1.99 us
  local copies, waits for them, and re-layouts: 1.88 us -> 0.01 us
  Pallas kernels: 19.4 us -> 17.6 us
    convert_element_type x0 -> x1, other arithmetic: none -> 1.99 us  [local(): return (lf.astype(F32) + angular.astype(F32)).astype(BF16)]
    unnamed x1 -> x2, local copies, waits for them, and re-layouts: 1.88 us -> 0.01 us
    pallas_call x1, Pallas kernels: 19.4 us -> 17.6 us  [local(): pl.pallas_call(functools.partial(kernel, lon_count, view_count), out_shap...]
where the time goes in v2:
time: 19.7 us; the launch traced here: 19.6 us
  Pallas kernels  17.6 us (89%)
  other arithmetic  1.99 us (10%)
    pallas_call x1, Pallas kernels, local(): pl.pallas_call(functools.partial(kernel, lon_count, view_count), out_shap...  17.6 us
    convert_element_type x1, other arithmetic, local(): return (lf.astype(F32) + angular.astype(F32)).astype(BF16)  1.99 us

profile of v2, /device:TPU:1, one launch (start us, length us, event | category | flops | bytes accessed | tf_op | source)
XLA Modules:
  0.0 19.6 jit_solution(9063311314680015950)
XLA Ops:
  0.0 0.0 copy-start
  0.0 17.6 %shard_map.55 = bf16[16,4,32,128]{3,2,1,0:T(8,128)(2,1)} custom-call(bf16[16,4,32,128]{3,2,1,0:T(8,128)(2,1)} %lf.1, bf16[3,3,3,128,128]{4,3,2,1,0:T(8,128)(2,1)} %sw.1, f32[3,128]{1,0:T(4,128)} %so_hbm.1, bf16[3,3,128,128]{3,2,1,0:T(8,128)(2,1)} %aw.1, f32[1,128]{1,0:T(1,128)} %bitcast.1), custom_call_target="tpu_custom_call" | custom-call | tf_op jit(solution)/shard_map/pallas_call | solution.py:267
  17.6 0.0 copy-done
  17.6 2.0 %add_convert_fusion = bf16[16,4,32,128]{3,2,1,0:T(8,128)(2,1)} fusion(bf16[16,4,32,128]{3,2,1,0:T(8,128)(2,1)} %shard_map.55, bf16[16,4,32,128]{3,2,1,0:T(8,128)(2,1)S(1)} %copy-done), kind=kLoop, calls=%fused_computation | loop fusion | flops 1048576 | bytes 1572864 | tf_op jit(solution)/shard_map/convert_element_type | solution.py:298
Async XLA Ops:
  0.0 17.6 %copy-start = (bf16[16,4,32,128]{3,2,1,0:T(8,128)(2,1)S(1)}, bf16[16,4,32,128]{3,2,1,0:T(8,128)(2,1)}, u32[]{:S(2)}) copy-start(bf16[16,4,32,128]{3,2,1,0:T(8,128)(2,1)} %lf.1) | copy-start | bytes 1572868

commit v3 on v2

--- a/solution.py
+++ b/solution.py
@@ -147,19 +147,6 @@
             for _, down in copies:
                 down.wait_recv()
 
-    for copy in biases:
-        copy.wait()
-    for copy in weights[0]:
-        copy.wait()
-    for p in range(pairs):
-        for h, value in enumerate(inner(0, x0, p, 3, cols + 1)):
-            x1[2 * p + h + 1, 3 * views:(cols + 1) * views, :] = value.astype(BF16)
-    for copy in weights[1]:
-        copy.wait()
-    for p in range(pairs):
-        for h, value in enumerate(inner(1, x1, p, 3, cols - 1)):
-            x2[2 * p + h + 1, 3 * views:(cols - 1) * views, :] = value.astype(BF16)
-
     pl.semaphore_wait(barrier, 2 + has_low.astype(jnp.int32) + has_high.astype(jnp.int32))
     to_left = pltpu.make_async_remote_copy(
         src_ref=x0.at[1:rows + 1, 3 * views:6 * views],
@@ -172,6 +159,19 @@
         device_id={"lon": right}, device_id_type=pl.DeviceIdType.MESH)
     to_left.start()
     to_right.start()
+
+    for copy in biases:
+        copy.wait()
+    for copy in weights[0]:
+        copy.wait()
+    for p in range(pairs):
+        for h, value in enumerate(inner(0, x0, p, 3, cols + 1)):
+            x1[2 * p + h + 1, 3 * views:(cols + 1) * views, :] = value.astype(BF16)
+    for copy in weights[1]:
+        copy.wait()
+    for p in range(pairs):
+        for h, value in enumerate(inner(1, x1, p, 3, cols - 1)):
+            x2[2 * p + h + 1, 3 * views:(cols - 1) * views, :] = value.astype(BF16)
 
     for copy in weights[2]:
         copy.wait()

time: 19.7 us -> 17.7 us (0.90)
  Pallas kernels: 17.6 us -> 15.5 us
    pallas_call x1, Pallas kernels: 17.6 us -> 15.5 us  [local(): pl.pallas_call(functools.partial(kernel, lon_count, view_count), out_shap...]
where the time goes in v3:
time: 17.7 us; the launch traced here: 17.6 us
  Pallas kernels  15.5 us (88%)
  other arithmetic  1.99 us (11%)
    pallas_call x1, Pallas kernels, local(): pl.pallas_call(functools.partial(kernel, lon_count, view_count), out_shap...  15.5 us
    convert_element_type x1, other arithmetic, local(): return (lf.astype(F32) + angular.astype(F32)).astype(BF16)  1.99 us

profile of v3, /device:TPU:1, one launch (start us, length us, event | category | flops | bytes accessed | tf_op | source)
XLA Modules:
  0.0 17.6 jit_solution(6618846450625976140)
XLA Ops:
  0.0 0.0 copy-start
  0.0 15.5 %shard_map.55 = bf16[16,4,32,128]{3,2,1,0:T(8,128)(2,1)} custom-call(bf16[16,4,32,128]{3,2,1,0:T(8,128)(2,1)} %lf.1, bf16[3,3,3,128,128]{4,3,2,1,0:T(8,128)(2,1)} %sw.1, f32[3,128]{1,0:T(4,128)} %so_hbm.1, bf16[3,3,128,128]{3,2,1,0:T(8,128)(2,1)} %aw.1, f32[1,128]{1,0:T(1,128)} %bitcast.1), custom_call_target="tpu_custom_call" | custom-call | tf_op jit(solution)/shard_map/pallas_call | solution.py:267
  15.5 0.0 copy-done
  15.6 2.0 %add_convert_fusion = bf16[16,4,32,128]{3,2,1,0:T(8,128)(2,1)} fusion(bf16[16,4,32,128]{3,2,1,0:T(8,128)(2,1)} %shard_map.55, bf16[16,4,32,128]{3,2,1,0:T(8,128)(2,1)S(1)} %copy-done), kind=kLoop, calls=%fused_computation | loop fusion | flops 1048576 | bytes 1572864 | tf_op jit(solution)/shard_map/convert_element_type | solution.py:298
Async XLA Ops:
  0.0 15.6 %copy-start = (bf16[16,4,32,128]{3,2,1,0:T(8,128)(2,1)S(1)}, bf16[16,4,32,128]{3,2,1,0:T(8,128)(2,1)}, u32[]{:S(2)}) copy-start(bf16[16,4,32,128]{3,2,1,0:T(8,128)(2,1)} %lf.1) | copy-start | bytes 1572868

commit v4 on v3

--- a/solution.py
+++ b/solution.py
@@ -237,10 +237,10 @@
                 jnp.concatenate(both, axis=0).astype(BF16))
     last_sent = view_copies(hid_edge, pairs, slice(0, 2 * EDGE * rows))
 
+    for u, q in blocks:
+        acc_edge[u, q] = partial(hid_edge, u, q, True)
     receive(sent)
     finish(hid, acc, put_middle)
-    for u, q in blocks:
-        acc_edge[u, q] = partial(hid_edge, u, q, True)
     receive([last_sent])
     finish(hid_edge, acc_edge, put_edge)
     for v in range(views):

time: 17.7 us -> 17.7 us (level)
  no operation moved by 1% of the time
where the time goes in v4:
time: 17.7 us; the launch traced here: 17.6 us
  Pallas kernels  15.5 us (88%)
  other arithmetic  1.99 us (11%)
    pallas_call x1, Pallas kernels, local(): pl.pallas_call(functools.partial(kernel, lon_count, view_count), out_shap...  15.5 us
    convert_element_type x1, other arithmetic, local(): return (lf.astype(F32) + angular.astype(F32)).astype(BF16)  1.99 us

profile of v4, /device:TPU:1, one launch (start us, length us, event | category | flops | bytes accessed | tf_op | source)
XLA Modules:
  0.0 17.6 jit_solution(8078142063592736058)
XLA Ops:
  0.0 0.0 copy-start
  0.0 15.5 %shard_map.55 = bf16[16,4,32,128]{3,2,1,0:T(8,128)(2,1)} custom-call(bf16[16,4,32,128]{3,2,1,0:T(8,128)(2,1)} %lf.1, bf16[3,3,3,128,128]{4,3,2,1,0:T(8,128)(2,1)} %sw.1, f32[3,128]{1,0:T(4,128)} %so_hbm.1, bf16[3,3,128,128]{3,2,1,0:T(8,128)(2,1)} %aw.1, f32[1,128]{1,0:T(1,128)} %bitcast.1), custom_call_target="tpu_custom_call" | custom-call | tf_op jit(solution)/shard_map/pallas_call | solution.py:267
  15.5 0.0 copy-done
  15.6 2.0 %add_convert_fusion = bf16[16,4,32,128]{3,2,1,0:T(8,128)(2,1)} fusion(bf16[16,4,32,128]{3,2,1,0:T(8,128)(2,1)} %shard_map.55, bf16[16,4,32,128]{3,2,1,0:T(8,128)(2,1)S(1)} %copy-done), kind=kLoop, calls=%fused_computation | loop fusion | flops 1048576 | bytes 1572864 | tf_op jit(solution)/shard_map/convert_element_type | solution.py:298
Async XLA Ops:
  0.0 15.6 %copy-start = (bf16[16,4,32,128]{3,2,1,0:T(8,128)(2,1)S(1)}, bf16[16,4,32,128]{3,2,1,0:T(8,128)(2,1)}, u32[]{:S(2)}) copy-start(bf16[16,4,32,128]{3,2,1,0:T(8,128)(2,1)} %lf.1) | copy-start | bytes 1572868
